TPU v7x, 32 devices: a whole 2x2x4 slice. The times are simulated.
32 devices in a mesh: groups: 2 (over x), shot: 16 (over z, y, core).
Axes of the slice: x: 2, y: 2, z: 4, core: 2. Of those that a mesh axis runs over, the one named last changes fastest.
Arguments:
- spectra: bfloat16 [1024, 2, 64, 512], P(('groups', 'shot')), parts along dimension 0, may hold values from -1.1953125 to 1.1953125
- fold_counts: int32 [1024], P('groups'), parts along dimension 0, may hold values from 1 to 512
- inverse_wavelet: float32 [2, 64], replicated, may hold values from -4 to 4
Outputs:
- multiples: bfloat16 [1024, 2, 64, 512], P(('groups', 'shot')), parts along dimension 0
There are 2 independent parts, one for each index of `groups`. A program takes and returns all parts, laid end to end along the dimension named above; an argument that names none is the same for every part. Nothing has to cross between parts.
All inputs are finite; a program needn't handle non-finite values.
Results may differ from a plain program's by a relative error of at most 0.001.
Values may be sent and summed in bfloat16 or wider, within the bound.
A program may use at most 64 MiB of HBM per device.

v0:
```python
import jax
import jax.numpy as jnp
from jax import lax
from jax.sharding import PartitionSpec as P


def batched_product(left_operand, right_operand):
    return jnp.einsum(
        "hwi,iwc->hwc", left_operand, right_operand, preferred_element_type=jnp.float32
    )


def shards(spectra, fold_counts, inverse_wavelet):
    points = spectra.shape[3]
    everyone = jnp.arange(points, dtype=jnp.int32)
    regrouped = lax.all_to_all(spectra, "shot", split_axis=2, concat_axis=0, tiled=True)
    recorded = jnp.abs(everyone[None, :] - everyone[:, None]) < fold_counts[:, None]
    flipped = regrouped.transpose(3, 1, 2, 0)
    regrouped = jnp.where(
        recorded[:, None, None, :],
        regrouped,
        jnp.where(recorded.T[:, None, None, :], flipped, jnp.zeros_like(regrouped)),
    )
    local_bins = regrouped.shape[2]
    real_component = regrouped[:, 0]
    imaginary_component = regrouped[:, 1]
    prod_real = batched_product(real_component, real_component) - batched_product(
        imaginary_component, imaginary_component
    )
    prod_imag = batched_product(real_component, imaginary_component) + batched_product(
        imaginary_component, real_component
    )
    first_bin = lax.axis_index("shot") * local_bins
    wave = lax.dynamic_slice_in_dim(inverse_wavelet, first_bin, local_bins, 1)
    wavelet_real = wave[0][None, :, None]
    wave_imag = wave[1][None, :, None]
    output_real = -(wavelet_real * prod_real - wave_imag * prod_imag)
    out_imag = -(wavelet_real * prod_imag + wave_imag * prod_real)
    result = jnp.stack([output_real, out_imag], axis=1).astype(jnp.bfloat16)
    return lax.all_to_all(result, "shot", split_axis=0, concat_axis=2, tiled=True)


def solution(mesh):
    in_specs = (P(("groups", "shot"), None, None, None), P("groups"), P())
    out_specs = P(("groups", "shot"), None, None, None)
    return jax.shard_map(shards, mesh=mesh, in_specs=in_specs, out_specs=out_specs, check_vma=False)
```

profile of v0, /device:TPU:13, one launch (start us, length us, event | category | flops | bytes accessed | tf_op | source)
XLA Modules:
  0.0 244.4 jit_solution(15204879253858754187)
XLA Ops:
  0.0 0.0 copy-start
  0.0 6.6 %copy.27 = bf16[32,2,64,512]{3,0,1,2:T(8,128)(2,1)} copy(bf16[32,2,64,512]{3,2,1,0:T(8,128)(2,1)} %param.3) | data formatting | bytes 8388608 | tf_op args[0]
  6.6 0.0 copy-start.2
  6.6 6.7 %all-to-all-start = ((bf16[32,2,64,512]{3,0,1,2:T(8,128)(2,1)}), bf16[32,2,64,512]{3,0,1,2:T(8,128)(2,1)}, u32[]{:S(2)}, u32[]{:S(2)}) async-start(bf16[32,2,64,512]{3,0,1,2:T(8,128)(2,1)} %copy.27), calls=%async_computation | async-start | bytes 8388608 | tf_op jit(solution)/shard_map/all_to_all | solution.py:16
  13.2 0.0 copy-done
  13.3 0.1 constant_dynamic-slice_fusion
  13.3 0.0 copy-done.2
  13.3 0.5 abs_compare_fusion.1
  13.8 91.9 %all-to-all-done = bf16[32,2,64,512]{3,0,1,2:T(8,128)(2,1)} async-done(((bf16[32,2,64,512]{3,0,1,2:T(8,128)(2,1)}), bf16[32,2,64,512]{3,0,1,2:T(8,128)(2,1)}, u32[]{:S(2)}, u32[]{:S(2)}) %all-to-all-start) | async-done | bytes 4194336 | tf_op jit(solution)/shard_map/all_to_all | solution.py:16
  105.7 4.8 %copy.29 = bf16[16,32,2,4,512]{4,1,0,3,2:T(8,128)(2,1)} copy(bf16[16,32,2,4,512]{4,1,2,3,0:T(8,128)(2,1)} %bitcast.3) | data formatting | bytes 8388608 | tf_op jit(solution)/shard_map/all_to_all | solution.py:16
  110.5 7.3 %copy.30 = bf16[512,2,4,512]{0,3,2,1:T(8,128)(2,1)} copy(bf16[512,2,4,512]{3,0,2,1:T(8,128)(2,1)} %bitcast.37) | data formatting | bytes 8388608 | tf_op jit(solution)/shard_map/all_to_all | solution.py:16
  117.8 5.1 %fusion = bf16[512,2,4,512]{3,0,2,1:T(8,128)(2,1)S(1)} fusion(bf16[512,2,4,512]{0,3,2,1:T(8,128)(2,1)} %copy.30, pred[512,512]{1,0:T(8,128)(4,1)S(1)} %get-tuple-element.8, pred[512,512]{1,0:T(8,128)(4,1)S(1)} %get-tuple-element.7, bf16[16,32,2,4,512]{4,1,0,3,2:T(8,128)(2,1)} %copy.29), kind=kLoop, calls=%fused_computation.2 | loop fusion | flops 4194304 | bytes 13107200 | tf_op jit(solution)/shard_map/jit(_where)/select_n | solution.py:19
  122.9 1.5 fusion.3
  124.4 1.5 fusion.4
  126.0 1.6 convolution_add_fusion
  127.5 2.9 %fusion.1 = (bf16[512,1,4,512]{0,3,2,1:T(8,128)(2,1)S(1)}, bf16[512,1,4,512]{0,3,2,1:T(8,128)(2,1)S(1)}) fusion(f32[4,512,512]{2,1,0:T(8,128)S(1)} %convolution_add_fusion, f32[4]{0:T(128)S(1)} %get-tuple-element.10, f32[4]{0:T(128)S(1)} %get-tuple-element.9, f32[4,512,512]{2,1,0:T(8,128)S(1)} %fusion.4, bf16[512,2,4,512]{3,0,2,1:T(8,128)(2,1)S(1)} %fusion), kind=kOutput, calls=%fused_computation.7 | convolution fusion | flops 1085276160 | bytes 14681088 | tf_op jit(solution)/shard_map/hwi,iwc->hwc/dot_general | solution.py:8
  130.5 2.4 pad_maximum_fusion
  132.9 7.9 %copy.35 = bf16[512,2,4,512]{3,2,1,0:T(4,128)(2,1)} copy(bf16[512,2,4,512]{0,3,2,1:T(8,128)(2,1)} %pad_maximum_fusion) | data formatting | bytes 8388608 | tf_op jit(solution)/shard_map/stack | solution.py:39
  140.7 97.2 %all_to_all.36 = bf16[512,2,4,512]{3,2,1,0:T(4,128)(2,1)S(1)} all-to-all(bf16[512,2,4,512]{3,2,1,0:T(4,128)(2,1)} %copy.35), channel_id=1, replica_groups=mesh['groups'=2,'shot'=16] {'shot'}, dimensions={0} | all-to-all | bytes 8388608 | tf_op jit(solution)/shard_map/all_to_all | solution.py:40
  237.9 1.5 copy.36
  239.4 0.6 copy.37
  240.0 0.0 copy-start.1
  240.0 4.4 %copy.38 = bf16[32,2,64,512]{3,2,1,0:T(8,128)(2,1)} copy(bf16[32,2,64,512]{3,0,2,1:T(8,128)(2,1)S(1)} %bitcast.39) | data formatting | bytes 8388608 | tf_op jit(solution)/shard_map/all_to_all | solution.py:40
  244.4 0.0 copy-done.1
  (1 shorter events, 0.0 us)
Async XLA Ops:
  0.0 13.2 %copy-start = (f32[2,64]{1,0:T(2,128)S(1)}, f32[2,64]{1,0:T(2,128)}, u32[]{:S(2)}) copy-start(f32[2,64]{1,0:T(2,128)} %param.5) | copy-start | bytes 1540
  6.6 6.8 %copy-start.2 = (s32[512]{0:T(512)S(1)}, s32[512]{0:T(512)}, u32[]{:S(2)}) copy-start(s32[512]{0:T(512)} %param.4) | copy-start | bytes 6148
  6.6 99.2 %all-to-all-start = ((bf16[32,2,64,512]{3,0,1,2:T(8,128)(2,1)}), bf16[32,2,64,512]{3,0,1,2:T(8,128)(2,1)}, u32[]{:S(2)}, u32[]{:S(2)}) async-start(bf16[32,2,64,512]{3,0,1,2:T(8,128)(2,1)} %copy.27), calls=%async_computation | async-start | bytes 8388608 | tf_op jit(solution)/shard_map/all_to_all | solution.py:16
  240.0 4.4 %copy-start.1 = (f32[2,64]{1,0:T(2,128)S(1)}, f32[2,64]{1,0:T(2,128)}, u32[]{:S(2)}) copy-start(f32[2,64]{1,0:T(2,128)} %param.5) | copy-start | bytes 1540
where the time goes:
time: 246 us; the launch traced here: 244 us
  blocking collectives  97.2 us (40%)
  waiting for transfers between devices  91.9 us (37%)
  local copies, waits for them, and re-layouts  33.1 us (13%)
  other arithmetic  8 us (3%)
  matrix products  7.55 us (3%)
  starting transfers between devices  6.69 us (3%)
    all_to_all x1, blocking collectives, shards(): lax.all_to_all(result, 'shot', split_axis=0, concat_axis=2, tiled=True)  97.2 us
    all_to_all x1, waiting for transfers between devices, shards(): lax.all_to_all(spectra, 'shot', split_axis=2, concat_axis=0, tiled=True)  91.9 us
    all_to_all x2, local copies, waits for them, and re-layouts, shards(): lax.all_to_all(spectra, 'shot', split_axis=2, concat_axis=0, tiled=True)  12.1 us
    another operation x1, local copies, waits for them, and re-layouts, shards(): result = jnp.stack([output_real, out_imag], axis=1).astype(jnp.bfloat16)  7.87 us
    dot_general x4, matrix products, batched_product(): jnp.einsum('hwi,iwc->hwc', left_operand, right_operand, preferred_element...  7.55 us
    all_to_all x1, starting transfers between devices, shards(): lax.all_to_all(spectra, 'shot', split_axis=2, concat_axis=0, tiled=True)  6.69 us
    unnamed x7, local copies, waits for them, and re-layouts  6.57 us
    all_to_all x3, local copies, waits for them, and re-layouts, shards(): lax.all_to_all(result, 'shot', split_axis=0, concat_axis=2, tiled=True)  6.48 us
  transfers between devices with their start and end apart: 1, of which 1 were waited for; matrix products, arithmetic and copies ran while one was open for 0% of the time, Pallas kernels for 0%

commit v1 on v0

v1 whole, which is shorter than its diff:
```python
import functools

import jax
import jax.numpy as jnp
from jax import lax
from jax.experimental import pallas as pl
from jax.experimental.pallas import tpu as pltpu
from jax.sharding import PartitionSpec as P

MESH = pl.DeviceIdType.MESH
VMEM_BYTES = 56 * 1024 * 1024


def exchange_kernel(n, x_ref, col_ref, row_ref, wave_ref, o_ref,
                    stage, send, recv, prod, landed, keep, swap, eye,
                    in_send, in_recv, out_send, out_recv, own_out, load_sem):
    shots, _, bins, points = x_ref.shape
    local = bins // n
    me = lax.axis_index("shot")
    mine = pl.ds(pl.multiple_of(me * shots, shots), shots)
    barrier = pltpu.get_barrier_semaphore()

    @pl.loop(1, n)
    def _(k):
        pl.semaphore_signal(barrier, inc=1, device_id={"shot": lax.rem(me + k, n)}, device_id_type=MESH)

    @pl.loop(0, shots)
    def _(s):
        rows = x_ref[s].reshape(2 * bins, points).astype(jnp.float32)
        for q in range(points // 128):
            stage[q, pl.ds(pl.multiple_of(s * 2 * bins, 2 * bins), 2 * bins), :] = rows[:, q * 128 : q * 128 + 128]

    @pl.loop(0, bins)
    def _(f):
        for c in range(2):
            for q in range(points // 128):
                lanes = pl.ds(q * 128, 128)
                send[f, c, :, lanes] = stage[q, pl.ds(c * bins + f, shots, stride=2 * bins), :].astype(jnp.bfloat16)

    pl.semaphore_wait(barrier, n - 1)

    @pl.loop(0, local)
    def _(j):
        pltpu.make_async_copy(send.at[me * local + j], recv.at[j, :, mine, :], in_recv.at[j]).start()

        @pl.loop(1, n)
        def _(k):
            to = lax.rem(me + k, n)
            pltpu.make_async_remote_copy(
                send.at[to * local + j], recv.at[j, :, mine, :], in_send, in_recv.at[j],
                device_id={"shot": to}, device_id_type=MESH).start()

    shot = lax.broadcasted_iota(jnp.int32, (points, points), 0)
    point = lax.broadcasted_iota(jnp.int32, (points, points), 1)
    apart = jnp.abs(shot - point)
    direct = apart < col_ref[...]
    mirrored = apart < row_ref[...]
    keep[...] = jnp.where(direct, 1.0, 0.0).astype(jnp.bfloat16)
    swap[...] = jnp.where(jnp.logical_and(direct, jnp.logical_not(mirrored)), 1.0, 0.0).astype(jnp.bfloat16)
    eye[...] = jnp.where(shot == point, 1.0, 0.0).astype(jnp.bfloat16)

    @pl.loop(0, local)
    def _(j):
        pltpu.make_async_copy(recv.at[j], recv.at[j], in_recv.at[j]).wait()
        for c in range(2):
            block = recv[j, c]
            turned = lax.dot_general(eye[...], block * swap[...], (((1,), (1,)), ((), ())),
                                     preferred_element_type=jnp.float32).astype(jnp.bfloat16)
            recv[j, c] = block * keep[...] + turned
        wave_real = wave_ref[0, me * local + j]
        wave_imag = wave_ref[1, me * local + j]
        tile = min(points, 256)

        @pl.loop(0, points // tile)
        def _(t):
            part = pl.ds(pl.multiple_of(t * tile, tile), tile)
            left_real, left_imag = recv[j, 0, part, :], recv[j, 1, part, :]
            real, imag = recv[j, 0], recv[j, 1]
            dot = functools.partial(jnp.dot, preferred_element_type=jnp.float32)
            prod_real = dot(left_real, real) - dot(left_imag, imag)
            prod_imag = dot(left_real, imag) + dot(left_imag, real)
            prod[j, 0, part, :] = (-(wave_real * prod_real - wave_imag * prod_imag)).astype(jnp.bfloat16)
            prod[j, 1, part, :] = (-(wave_real * prod_imag + wave_imag * prod_real)).astype(jnp.bfloat16)

        pltpu.make_async_copy(prod.at[j, :, mine, :], landed.at[me * local + j], own_out).start()

        @pl.loop(1, n)
        def _(k):
            to = lax.rem(me + k, n)
            theirs = pl.ds(pl.multiple_of(to * shots, shots), shots)
            pltpu.make_async_remote_copy(
                prod.at[j, :, theirs, :], landed.at[me * local + j], out_send, out_recv,
                device_id={"shot": to}, device_id_type=MESH).start()

    others = pl.ds(0, (n - 1) * local)
    pltpu.make_async_copy(landed.at[pl.ds(0, local)], landed.at[pl.ds(0, local)], own_out).wait()
    pltpu.make_async_copy(send.at[others], send.at[others], in_send).wait()
    pltpu.make_async_copy(landed.at[others], landed.at[others], out_send).wait()
    pltpu.make_async_copy(landed.at[others], landed.at[others], out_recv).wait()
    out = pltpu.make_async_copy(landed, o_ref, load_sem)
    out.start()
    out.wait()


def shards(n, spectra, fold_counts, inverse_wavelet):
    shots, _, bins, points = spectra.shape
    local = bins // n
    vmem = pl.BlockSpec(memory_space=pltpu.VMEM)
    bf16 = jnp.bfloat16
    landed = pl.pallas_call(
        functools.partial(exchange_kernel, n),
        out_shape=jax.ShapeDtypeStruct((bins, 2, shots, points), bf16),
        in_specs=[vmem, vmem, vmem, pl.BlockSpec(memory_space=pltpu.SMEM)],
        out_specs=pl.BlockSpec(memory_space=pl.ANY),
        scratch_shapes=[
            pltpu.VMEM((points // 128, shots * 2 * bins, 128), jnp.float32),
            pltpu.VMEM((bins, 2, shots, points), bf16),
            pltpu.VMEM((local, 2, points, points), bf16),
            pltpu.VMEM((local, 2, points, points), bf16),
            pltpu.VMEM((bins, 2, shots, points), bf16),
            pltpu.VMEM((points, points), bf16),
            pltpu.VMEM((points, points), bf16),
            pltpu.VMEM((points, points), bf16),
            pltpu.SemaphoreType.DMA,
            pltpu.SemaphoreType.DMA((local,)),
            pltpu.SemaphoreType.DMA,
            pltpu.SemaphoreType.DMA,
            pltpu.SemaphoreType.DMA,
            pltpu.SemaphoreType.DMA,
        ],
        compiler_params=pltpu.CompilerParams(
            collective_id=0, has_side_effects=True, vmem_limit_bytes=VMEM_BYTES),
    )(spectra, fold_counts[:, None], fold_counts[None, :], inverse_wavelet)
    return landed.transpose(2, 1, 0, 3)


def solution(mesh):
    spec = P(("groups", "shot"), None, None, None)
    return jax.shard_map(functools.partial(shards, mesh.shape["shot"]), mesh=mesh,
                         in_specs=(spec, P("groups"), P()), out_specs=spec, check_vma=False)
```

time: 246 us -> 205 us (0.83)
  Pallas kernels: 0 us -> 197 us
  blocking collectives: 97.2 us -> 0 us
  waiting for transfers between devices: 91.9 us -> 0 us
  local copies, waits for them, and re-layouts: 33.1 us -> 8.08 us
  other arithmetic: 8 us -> 0 us
  matrix products: 7.55 us -> 0 us
  starting transfers between devices: 6.69 us -> 0 us
    pallas_call x0 -> x1, Pallas kernels: none -> 197 us  [shards(): pl.pallas_call(functools.partial(exchange_kernel, n), out_shape=jax.Shape...]
    all_to_all x1 -> x0, blocking collectives: 97.2 us -> none  [shards(): lax.all_to_all(result, 'shot', split_axis=0, concat_axis=2, tiled=True)]
    all_to_all x1 -> x0, waiting for transfers between devices: 91.9 us -> none  [shards(): lax.all_to_all(spectra, 'shot', split_axis=2, concat_axis=0, tiled=True)]
    all_to_all x5 -> x0, local copies, waits for them, and re-layouts: 18.5 us -> none  [the longest x2 12.1 us: shards(): lax.all_to_all(spectra, 'shot', split_axis=2, concat_axis=0, tiled=True)]
    another operation x1 -> x0, local copies, waits for them, and re-layouts: 7.87 us -> none  [shards(): result = jnp.stack([output_real, out_imag], axis=1).astype(jnp.bfloat16)]
    dot_general x4 -> x0, matrix products: 7.55 us -> none  [batched_product(): jnp.einsum('hwi,iwc->hwc', left_operand, right_operand, preferred_element...]
    all_to_all x1 -> x0, starting transfers between devices: 6.69 us -> none  [shards(): lax.all_to_all(spectra, 'shot', split_axis=2, concat_axis=0, tiled=True)]
    unnamed x7 -> x0, local copies, waits for them, and re-layouts: 6.57 us -> none
  transfers between devices with their start and end apart: 1 -> 0, of which waited for: 1 -> 0; matrix products, arithmetic and copies ran while one was open for 0% -> 0% of each run, Pallas kernels for 0% -> 0%
where the time goes in v1:
time: 205 us
  Pallas kernels  197 us (96%)
  local copies, waits for them, and re-layouts  8.08 us (4%)
    pallas_call x1, Pallas kernels, shards(): pl.pallas_call(functools.partial(exchange_kernel, n), out_shape=jax.Shape...  197 us
    transpose x1, local copies, waits for them, and re-layouts, shards(): return landed.transpose(2, 1, 0, 3)  6.54 us

profile of v1, /device:TPU:13, one launch (start us, length us, event | category | flops | bytes accessed | tf_op | source)
XLA Modules:
  0.0 204.6 jit_solution(13007888706529148942)
XLA Ops:
  0.0 1.5 copy.5.col_ref
  1.5 196.5 %shard_map.37 = bf16[64,2,32,512]{3,2,1,0:T(8,128)(2,1)} custom-call(bf16[32,2,64,512]{3,2,1,0:T(8,128)(2,1)} %x_ref.1, s32[512,1]{1,0:T(8,128)} %copy.5.col_ref, s32[1,512]{1,0:T(1,128)} %bitcast.5, f32[2,64]{1,0:T(2,128)} %wave_ref.1), custom_call_target="tpu_custom_call" | custom-call | tf_op jit(solution)/shard_map/pallas_call | solution.py:110
  198.1 6.5 %copy.6 = bf16[32,2,64,512]{3,2,1,0:T(8,128)(2,1)} copy(bf16[32,2,64,512]{3,0,1,2:T(8,128)(2,1)} %bitcast.3) | data formatting | bytes 8388608 | tf_op jit(solution)/shard_map/transpose | solution.py:134

commit v2 on v1

v2 whole, which is shorter than its diff:
```python
import functools

import jax
import jax.numpy as jnp
from jax import lax
from jax.experimental import pallas as pl
from jax.experimental.pallas import tpu as pltpu
from jax.sharding import PartitionSpec as P

MESH = pl.DeviceIdType.MESH
VMEM_BYTES = 56 * 1024 * 1024


def turn(eye, block):
    return lax.dot_general(eye, block, (((1,), (1,)), ((), ())),
                           preferred_element_type=jnp.float32).astype(jnp.bfloat16)


def exchange_kernel(n, x_hbm, row_ref, wave_ref, o_ref,
                    x_ref, stage, send, recv, prod, keep, swap, eye,
                    load_sem, own_in, in_send, in_recv, out_send, out_recv, own_out):
    shots, _, bins, points = x_ref.shape
    local = bins // n
    me = lax.axis_index("shot")
    mine = pl.ds(pl.multiple_of(me * shots, shots), shots)
    barrier = pltpu.get_barrier_semaphore()
    chunks = load_sem.shape[0]
    chunk = shots // chunks

    def load(i):
        rows = pl.ds(i * chunk, chunk)
        return pltpu.make_async_copy(x_hbm.at[rows], x_ref.at[rows], load_sem.at[i])

    for i in range(chunks):
        load(i).start()

    @pl.loop(1, n)
    def _(k):
        pl.semaphore_signal(barrier, inc=1, device_id={"shot": lax.rem(me + k, n)}, device_id_type=MESH)

    for i in range(chunks):
        load(i).wait()

        @pl.loop(i * chunk, (i + 1) * chunk)
        def _(s):
            rows = x_ref[s].reshape(2 * bins, points).astype(jnp.float32)
            for q in range(points // 128):
                stage[q, pl.ds(pl.multiple_of(s * 2 * bins, 2 * bins), 2 * bins), :] = rows[:, q * 128 : q * 128 + 128]

    def gather(f):
        for c in range(2):
            for q in range(points // 128):
                traces = stage[q, pl.ds(c * bins + f, shots, stride=2 * bins), :]
                send[f, c, :, pl.ds(q * 128, 128)] = traces.astype(jnp.bfloat16)

    pl.semaphore_wait(barrier, n - 1)

    @pl.loop(0, local)
    def _(j):
        @pl.loop(1, n)
        def _(k):
            to = lax.rem(me + k, n)
            gather(to * local + j)
            pltpu.make_async_remote_copy(
                send.at[to * local + j], recv.at[j, :, mine, :], in_send, in_recv.at[j],
                device_id={"shot": to}, device_id_type=MESH).start()

        gather(me * local + j)
        pltpu.make_async_copy(send.at[me * local + j], recv.at[j, :, mine, :], own_in.at[j]).start()

    shot = lax.broadcasted_iota(jnp.int32, (points, points), 0)
    point = lax.broadcasted_iota(jnp.int32, (points, points), 1)
    eye[...] = jnp.where(shot == point, 1.0, 0.0).astype(jnp.bfloat16)
    mirrored = jnp.where(jnp.abs(shot - point) < row_ref[...], 1.0, 0.0).astype(jnp.bfloat16)
    keep[...] = turn(eye[...], mirrored)
    swap[...] = keep[...] * (1.0 - mirrored)

    @pl.loop(0, local)
    def _(j):
        pltpu.make_async_copy(send.at[me * local + j], recv.at[j, :, mine, :], own_in.at[j]).wait()
        rest = pl.ds(0, (n - 1) * shots)
        pltpu.make_async_copy(recv.at[j, :, rest, :], recv.at[j, :, rest, :], in_recv.at[j]).wait()
        for c in range(2):
            block = recv[j, c]
            recv[j, c] = block * keep[...] + turn(eye[...], block * swap[...])
        wave_real = wave_ref[0, me * local + j]
        wave_imag = wave_ref[1, me * local + j]
        tile = min(points, 256)

        @pl.loop(0, points // tile)
        def _(t):
            part = pl.ds(pl.multiple_of(t * tile, tile), tile)
            left_real, left_imag = recv[j, 0, part, :], recv[j, 1, part, :]
            real, imag = recv[j, 0], recv[j, 1]
            dot = functools.partial(jnp.dot, preferred_element_type=jnp.float32)
            prod_real = dot(left_real, real) - dot(left_imag, imag)
            prod_imag = dot(left_real, imag) + dot(left_imag, real)
            prod[j, 0, part, :] = (-(wave_real * prod_real - wave_imag * prod_imag)).astype(jnp.bfloat16)
            prod[j, 1, part, :] = (-(wave_real * prod_imag + wave_imag * prod_real)).astype(jnp.bfloat16)

        pltpu.make_async_copy(prod.at[j, :, mine, :], o_ref.at[me * local + j], own_out).start()

        @pl.loop(1, n)
        def _(k):
            to = lax.rem(me + k, n)
            theirs = pl.ds(pl.multiple_of(to * shots, shots), shots)
            pltpu.make_async_remote_copy(
                prod.at[j, :, theirs, :], o_ref.at[me * local + j], out_send, out_recv,
                device_id={"shot": to}, device_id_type=MESH).start()

    others = pl.ds(0, (n - 1) * local)
    pltpu.make_async_copy(o_ref.at[pl.ds(0, local)], o_ref.at[pl.ds(0, local)], own_out).wait()
    pltpu.make_async_copy(send.at[others], send.at[others], in_send).wait()
    pltpu.make_async_copy(o_ref.at[others], o_ref.at[others], out_send).wait()
    pltpu.make_async_copy(o_ref.at[others], o_ref.at[others], out_recv).wait()

def regroup_kernel(x_ref, o_ref, stage):
    bins, _, shots, points = x_ref.shape

    @pl.loop(0, bins)
    def _(f):
        rows = x_ref[f, 0].astype(jnp.float32)
        for q in range(points // 128):
            stage[q, pl.ds(pl.multiple_of(f * shots, shots), shots), :] = rows[:, q * 128 : q * 128 + 128]

    @pl.loop(0, shots)
    def _(s):
        for q in range(points // 128):
            o_ref[s, 0, :, pl.ds(q * 128, 128)] = stage[q, pl.ds(s, bins, stride=shots), :].astype(jnp.bfloat16)


def shards(n, spectra, fold_counts, inverse_wavelet):
    shots, _, bins, points = spectra.shape
    local = bins // n
    bf16 = jnp.bfloat16
    landed = pl.pallas_call(
        functools.partial(exchange_kernel, n),
        out_shape=jax.ShapeDtypeStruct((bins, 2, shots, points), bf16),
        in_specs=[pl.BlockSpec(memory_space=pl.ANY), pl.BlockSpec(memory_space=pltpu.VMEM),
                  pl.BlockSpec(memory_space=pltpu.SMEM)],
        out_specs=pl.BlockSpec(memory_space=pl.ANY),
        scratch_shapes=[
            pltpu.VMEM(spectra.shape, bf16),
            pltpu.VMEM((points // 128, shots * 2 * bins, 128), jnp.float32),
            pltpu.VMEM((bins, 2, shots, points), bf16),
            pltpu.VMEM((local, 2, points, points), bf16),
            pltpu.VMEM((local, 2, points, points), bf16),
            pltpu.VMEM((points, points), bf16),
            pltpu.VMEM((points, points), bf16),
            pltpu.VMEM((points, points), bf16),
            pltpu.SemaphoreType.DMA((4,)),
            pltpu.SemaphoreType.DMA((local,)),
            pltpu.SemaphoreType.DMA,
            pltpu.SemaphoreType.DMA((local,)),
            pltpu.SemaphoreType.DMA,
            pltpu.SemaphoreType.DMA,
            pltpu.SemaphoreType.DMA,
        ],
        compiler_params=pltpu.CompilerParams(
            collective_id=0, has_side_effects=True, vmem_limit_bytes=VMEM_BYTES),
    )(spectra, fold_counts[None, :], inverse_wavelet)
    few = min(shots, 16)
    return pl.pallas_call(
        regroup_kernel,
        grid=(shots // few, 2),
        out_shape=jax.ShapeDtypeStruct(spectra.shape, bf16),
        in_specs=[pl.BlockSpec((bins, 1, few, points), lambda s, c: (0, c, s, 0))],
        out_specs=pl.BlockSpec((few, 1, bins, points), lambda s, c: (s, c, 0, 0)),
        scratch_shapes=[pltpu.VMEM((points // 128, bins * few, 128), jnp.float32)],
    )(landed)


def solution(mesh):
    spec = P(("groups", "shot"), None, None, None)
    return jax.shard_map(functools.partial(shards, mesh.shape["shot"]), mesh=mesh,
                         in_specs=(spec, P("groups"), P()), out_specs=spec, check_vma=False)
```

time: 205 us -> 196 us (0.956)
  local copies, waits for them, and re-layouts: 8.08 us -> 0 us
    pallas_call x1, Pallas kernels: 197 us -> 187 us  [shards(): pl.pallas_call(functools.partial(exchange_kernel, n), out_shape=jax.Shape...]
    pallas_call x0 -> x1, Pallas kernels: none -> 8.75 us  [shards(): pl.pallas_call(regroup_kernel, grid=(shots // few, 2), out_shape=jax.Shap...]
    transpose x1 -> x0, local copies, waits for them, and re-layouts: 6.54 us -> none  [shards(): return landed.transpose(2, 1, 0, 3)]
where the time goes in v2:
time: 196 us
  Pallas kernels  196 us (100%)
    pallas_call x1, Pallas kernels, shards(): pl.pallas_call(functools.partial(exchange_kernel, n), out_shape=jax.Shape...  187 us
    pallas_call x1, Pallas kernels, shards(): pl.pallas_call(regroup_kernel, grid=(shots // few, 2), out_shape=jax.Shap...  8.75 us

profile of v2, /device:TPU:13, one launch (start us, length us, event | category | flops | bytes accessed | tf_op | source)
XLA Modules:
  0.0 196.0 jit_solution(713283264860611096)
XLA Ops:
  0.0 187.3 %shard_map.37.x_ref = bf16[64,2,32,512]{3,2,1,0:T(8,128)(2,1)} custom-call(bf16[32,2,64,512]{3,2,1,0:T(8,128)(2,1)} %x_hbm.1, s32[1,512]{1,0:T(1,128)} %bitcast.1, f32[2,64]{1,0:T(2,128)} %wave_ref.1), custom_call_target="tpu_custom_call" | custom-call | tf_op jit(solution)/shard_map/pallas_call | solution.py:136
  187.3 8.7 %shard_map.38 = bf16[32,2,64,512]{3,2,1,0:T(8,128)(2,1)} custom-call(bf16[64,2,32,512]{3,2,1,0:T(8,128)(2,1)} %shard_map.37.x_ref), custom_call_target="tpu_custom_call" | custom-call | tf_op jit(solution)/shard_map/pallas_call | solution.py:163

commit v3 on v2

--- a/solution.py
+++ b/solution.py
@@ -114,19 +114,10 @@
     pltpu.make_async_copy(o_ref.at[others], o_ref.at[others], out_send).wait()
     pltpu.make_async_copy(o_ref.at[others], o_ref.at[others], out_recv).wait()
 
-def regroup_kernel(x_ref, o_ref, stage):
-    bins, _, shots, points = x_ref.shape
-
-    @pl.loop(0, bins)
-    def _(f):
-        rows = x_ref[f, 0].astype(jnp.float32)
-        for q in range(points // 128):
-            stage[q, pl.ds(pl.multiple_of(f * shots, shots), shots), :] = rows[:, q * 128 : q * 128 + 128]
-
-    @pl.loop(0, shots)
-    def _(s):
-        for q in range(points // 128):
-            o_ref[s, 0, :, pl.ds(q * 128, 128)] = stage[q, pl.ds(s, bins, stride=shots), :].astype(jnp.bfloat16)
+def regroup_kernel(x_ref, o_ref):
+    for q in range(x_ref.shape[3] // 128):
+        lanes = pl.ds(q * 128, 128)
+        o_ref[:, 0, :, lanes] = jnp.swapaxes(x_ref[:, 0, :, lanes], 0, 1)
 
 
 def shards(n, spectra, fold_counts, inverse_wavelet):
@@ -166,7 +157,6 @@
         out_shape=jax.ShapeDtypeStruct(spectra.shape, bf16),
         in_specs=[pl.BlockSpec((bins, 1, few, points), lambda s, c: (0, c, s, 0))],
         out_specs=pl.BlockSpec((few, 1, bins, points), lambda s, c: (s, c, 0, 0)),
-        scratch_shapes=[pltpu.VMEM((points // 128, bins * few, 128), jnp.float32)],
     )(landed)
 
 

time: 196 us -> 193 us (0.985)
  Pallas kernels: 196 us -> 193 us
    pallas_call x1, Pallas kernels: 8.75 us -> 5.55 us  [shards(): pl.pallas_call(regroup_kernel, grid=(shots // few, 2), out_shape=jax.Shap...]
where the time goes in v3:
time: 193 us
  Pallas kernels  193 us (100%)
    pallas_call x1, Pallas kernels, shards(): pl.pallas_call(functools.partial(exchange_kernel, n), out_shape=jax.Shape...  187 us
    pallas_call x1, Pallas kernels, shards(): pl.pallas_call(regroup_kernel, grid=(shots // few, 2), out_shape=jax.Shap...  5.55 us

profile of v3, /device:TPU:13, one launch (start us, length us, event | category | flops | bytes accessed | tf_op | source)
XLA Modules:
  0.0 192.8 jit_solution(8676198752354547975)
XLA Ops:
  0.0 187.3 %shard_map.37.x_ref = bf16[64,2,32,512]{3,2,1,0:T(8,128)(2,1)} custom-call(bf16[32,2,64,512]{3,2,1,0:T(8,128)(2,1)} %x_hbm.1, s32[1,512]{1,0:T(1,128)} %bitcast.1, f32[2,64]{1,0:T(2,128)} %wave_ref.1), custom_call_target="tpu_custom_call" | custom-call | tf_op jit(solution)/shard_map/pallas_call | solution.py:127
  187.3 5.6 %shard_map.38 = bf16[32,2,64,512]{3,2,1,0:T(8,128)(2,1)} custom-call(bf16[64,2,32,512]{3,2,1,0:T(8,128)(2,1)} %shard_map.37.x_ref), custom_call_target="tpu_custom_call" | custom-call | tf_op jit(solution)/shard_map/pallas_call | solution.py:154
